TPU v7x, 32 devices: a whole 2x2x4 slice. The times are simulated.
32 devices in a mesh: rows: 4 (over z), cent: 8 (over y, x, core).
Axes of the slice: x: 2, y: 2, z: 4, core: 2. Of those that a mesh axis runs over, the one named last changes fastest.
Arguments:
- train_rows: float32 [16384, 64], P('rows'), may hold values from -6 to 6
- centre_index: int32 [16384], P('cent'), may hold values from 0 to 16383
- precond: bfloat16 [16384, 16384], P('cent', 'rows'), as said below
- coefficients: float32 [16384, 128], P(('rows', 'cent')), may hold values from -6 to 6
- residual: float32 [16384, 128], P(('rows', 'cent')), may hold values from -6 to 6
- direction: float32 [16384, 128], P(('rows', 'cent')), may hold values from -6 to 6
Outputs:
- coef_next: float32 [16384, 128], P(('rows', 'cent'))
- residual_next: float32 [16384, 128], P(('rows', 'cent'))
- direction_next: float32 [16384, 128], P(('rows', 'cent'))
Inputs may be any that keep to these rules, and one draw needn't show every extreme that they name: precond is zero below its diagonal.
All inputs are finite; a program needn't handle non-finite values.
Results may differ from a plain program's by a relative error of at most 0.0047.
Values may be sent and summed in bfloat16 or wider, within the bound.
A program may use at most 128 MiB of HBM per device.

v0:
```python
import math
import jax
import jax.numpy as jnp
from jax import lax
from jax.sharding import PartitionSpec as P

FEAT = 64
OUTS = 128
ridge_weight = 0.1


def kernel_tile(block_rows, centres):
    row_sq = jnp.sum(block_rows * block_rows, axis=1)
    cen_sq = jnp.sum(centres * centres, axis=1)
    cross = jnp.dot(
        block_rows, centres.T, precision=lax.Precision.HIGHEST, preferred_element_type=jnp.float32
    )
    distance = row_sq[:, None] + cen_sq[None, :] - 2.0 * cross
    return jnp.exp(-(2.0 / FEAT) * distance).astype(jnp.bfloat16)


def kernel_pass(local_rows, centres, coef_field, combine):
    count_rows = local_rows.shape[0]
    block_size = math.gcd(count_rows, 1024)
    block_count = count_rows // block_size
    groups = local_rows.reshape(block_count, block_size, FEAT)
    tiles = lax.map(lambda group_rows: kernel_tile(group_rows, centres), groups)
    fitted_part = jnp.einsum(
        "kbc,cd->kbd", tiles, coef_field, preferred_element_type=jnp.float32
    ).reshape(count_rows, OUTS)
    fitted = combine(fitted_part)
    fitted_groups = fitted.reshape(block_count, block_size, OUTS)
    grad_part = jnp.einsum("kbc,kbd->cd", tiles, fitted_groups, preferred_element_type=jnp.float32)
    return grad_part


def on_device(train_rows, centre_index, precond, coefficients, residual, direction):
    rows_here = train_rows.shape[0]
    start_row = lax.axis_index("rows") * rows_here
    offset = centre_index - start_row
    inside = ((offset >= 0) & (offset < rows_here)).astype(jnp.float32)
    picked = train_rows[jnp.clip(offset, 0, rows_here - 1)] * inside[:, None]
    centres = lax.psum(picked, "rows")
    dir_low = direction.astype(jnp.bfloat16)
    columns = precond
    partial_field = jnp.dot(
        columns,
        lax.all_gather(dir_low, "cent", axis=0, tiled=True),
        preferred_element_type=jnp.float32,
    )
    coef_field = lax.psum(partial_field, "rows").astype(jnp.bfloat16)

    def line_sum(part):
        return lax.psum(part, "cent").astype(jnp.bfloat16)

    grad_part = kernel_pass(train_rows, centres, coef_field, line_sum)
    grad = lax.psum(grad_part, "rows")
    grad_low = (grad * float(rows_here * lax.axis_size("rows")) ** (-0.5)).astype(jnp.bfloat16)
    columns = precond
    image = lax.psum_scatter(
        lax.dot_general(
            columns, grad_low, (((0,), (0,)), ((), ())), preferred_element_type=jnp.float32
        ),
        "cent",
        scatter_dimension=0,
        tiled=True,
    )
    image = image + ridge_weight * direction
    norm_old, curvature = lax.psum(
        (jnp.sum(residual * residual), jnp.sum(direction * image)), ("rows", "cent")
    )
    step_size = norm_old / curvature
    coef_next = coefficients + step_size * direction
    residual_next = residual - step_size * image
    norm_new = lax.psum(jnp.sum(residual_next * residual_next), ("rows", "cent"))
    direction_next = residual_next + norm_new / norm_old * direction
    return (coef_next, residual_next, direction_next)


def solution(mesh):
    placed = (
        P("rows", None),
        P("cent"),
        P("cent", "rows"),
        P(("rows", "cent"), None),
        P(("rows", "cent"), None),
        P(("rows", "cent"), None),
    )
    return jax.shard_map(
        on_device,
        mesh=mesh,
        in_specs=placed,
        out_specs=(P(("rows", "cent"), None), P(("rows", "cent"), None), P(("rows", "cent"), None)),
        check_vma=False,
    )
```

profile of v0, /device:TPU:0, one launch (start us, length us, event | category | flops | bytes accessed | tf_op | source)
XLA Modules:
  0.0 441.2 jit_solution(3471181950002680406)
XLA Ops:
  9.5 1.8 copy.9
  11.3 5.5 %gather_fusion = f32[2048,64]{1,0:T(8,128)S(1)} fusion(f32[4096,64]{1,0:T(8,128)S(1)} %copy.9, s32[2048]{0:T(1024)S(1)} %fusion.8), kind=kCustom, calls=%fused_computation | custom fusion | bytes 1056768 | tf_op jit(solution)/shard_map/gather | solution.py:42
  16.8 1.3 broadcast_multiply_fusion
  18.2 1.6 convert_element_type.21
  19.9 53.0 %all-reduce.6.cloned.1.call-done = f32[2048,64]{1,0:T(8,128)} async-done(((f32[2048,64]{1,0:T(8,128)}), f32[2048,64]{1,0:T(8,128)}) %all-reduce.6.cloned.1.call-update) | async-done | bytes 524304 | tf_op jit(solution)/shard_map/psum | solution.py:43
  72.9 1.6 multiply_reduce_fusion
  74.5 45.0 %while.12 = (s32[]{:T(128)}, bf16[4,1024,2048]{2,1,0:T(8,128)(2,1)}, f32[4,1024,64]{2,1,0:T(8,128)S(1)}, f32[2048]{0:T(1024)S(1)}, f32[2048,64]{1,0:T(8,128)}, /*index=5*/s32[]{:T(128)}) while((s32[]{:T(128)}, bf16[4,1024,2048]{2,1,0:T(8,128)(2,1)}, f32[4,1024,64]{2,1,0:T(8,128)S(1)}, f32[2048]{0:T(1024)S(1)}, f32[2048,64]{1,0:T(8,128)}, ...), condition=%wide.region_6.7_spmd, body=%wide.region_4.0_spmd.sunk | while | flops 1621228544 | bytes 6046793 | solution.py:27
  74.7 11.0 %bitcast_dynamic-update-slice_fusion.2 = bf16[4,1024,2048]{2,1,0:T(8,128)(2,1)} fusion(bf16[4,1024,2048]{2,1,0:T(8,128)(2,1)} %get-tuple-element.116, s32[]{:T(128)} %get-tuple-element.115, f32[2048,64]{1,0:T(8,128)} %get-tuple-element.125, f32[2048]{0:T(1024)S(1)} %get-tuple-element.124, f32[1024]{0:T(1024)S(1)} %fusion.23, ...), kind=kOutput, calls=%fused_computation.2.clone.1 | convolution fusion | flops 1621098496 | bytes 5780480 | tf_op jit(solution)/shard_map/while/body/eval_jaxpr/dot_general | solution.py:15
  85.9 11.1 %bitcast_dynamic-update-slice_fusion.2 = bf16[4,1024,2048]{2,1,0:T(8,128)(2,1)} fusion(bf16[4,1024,2048]{2,1,0:T(8,128)(2,1)} %get-tuple-element.116, s32[]{:T(128)} %get-tuple-element.115, f32[2048,64]{1,0:T(8,128)} %get-tuple-element.125, f32[2048]{0:T(1024)S(1)} %get-tuple-element.124, f32[1024]{0:T(1024)S(1)} %fusion.23, ...), kind=kOutput, calls=%fused_computation.2.clone.1 | convolution fusion | flops 1621098496 | bytes 5780480 | tf_op jit(solution)/shard_map/while/body/eval_jaxpr/dot_general | solution.py:15
  97.2 11.0 %bitcast_dynamic-update-slice_fusion.2 = bf16[4,1024,2048]{2,1,0:T(8,128)(2,1)} fusion(bf16[4,1024,2048]{2,1,0:T(8,128)(2,1)} %get-tuple-element.116, s32[]{:T(128)} %get-tuple-element.115, f32[2048,64]{1,0:T(8,128)} %get-tuple-element.125, f32[2048]{0:T(1024)S(1)} %get-tuple-element.124, f32[1024]{0:T(1024)S(1)} %fusion.23, ...), kind=kOutput, calls=%fused_computation.2.clone.1 | convolution fusion | flops 1621098496 | bytes 5780480 | tf_op jit(solution)/shard_map/while/body/eval_jaxpr/dot_general | solution.py:15
  108.4 11.1 %bitcast_dynamic-update-slice_fusion.2 = bf16[4,1024,2048]{2,1,0:T(8,128)(2,1)} fusion(bf16[4,1024,2048]{2,1,0:T(8,128)(2,1)} %get-tuple-element.116, s32[]{:T(128)} %get-tuple-element.115, f32[2048,64]{1,0:T(8,128)} %get-tuple-element.125, f32[2048]{0:T(1024)S(1)} %get-tuple-element.124, f32[1024]{0:T(1024)S(1)} %fusion.23, ...), kind=kOutput, calls=%fused_computation.2.clone.1 | convolution fusion | flops 1621098496 | bytes 5780480 | tf_op jit(solution)/shard_map/while/body/eval_jaxpr/dot_general | solution.py:15
  119.5 8.4 %fusion.10 = f32[2048,128]{1,0:T(8,128)S(1)} fusion(bf16[2048,4096]{1,0:T(8,128)(2,1)} %param.10, bf16[4096,128]{1,0:T(8,128)(2,1)} %all-gather.2.cloned.1.call-done), kind=kOutput, calls=%fused_computation.28 | convolution fusion | flops 2147483648 | bytes 18874368 | tf_op jit(solution)/shard_map/dot_general | solution.py:46
  127.9 41.5 %all-reduce.9 = bf16[2048,128]{1,0:T(8,128)(2,1)S(1)} all-reduce(f32[2048,128]{1,0:T(8,128)S(1)} %fusion.10), channel_id=1, replica_groups=mesh['rows'=4,'cent'=8] {'rows'}, use_global_device_ids=true, to_apply=%region_7.8 | all-reduce | flops 262144 | bytes 1572864 | tf_op jit(solution)/shard_map/psum | solution.py:51
  169.5 8.2 %fusion.4 = f32[4,1024,128]{2,1,0:T(8,128)S(1)} fusion(bf16[4,1024,2048]{2,1,0:T(8,128)(2,1)} %get-tuple-element.58, bf16[2048,128]{1,0:T(8,128)(2,1)S(1)} %all-reduce.9), kind=kOutput, calls=%fused_computation.12 | convolution fusion | flops 2147483648 | bytes 19398656 | tf_op jit(solution)/shard_map/kbc,cd->kbd/dot_general | solution.py:28
  177.6 56.6 %all-reduce.10 = bf16[4096,128]{1,0:T(8,128)(2,1)S(1)} all-reduce(f32[4096,128]{1,0:T(8,128)S(1)} %bitcast.34), channel_id=1, replica_groups=mesh['rows'=4,'cent'=8] {'cent'}, use_global_device_ids=true, to_apply=%region_8.9 | all-reduce | flops 524288 | bytes 3145728 | tf_op jit(solution)/shard_map/psum | solution.py:54
  234.2 9.2 %convolution_bitcast_fusion.1 = f32[2048,128]{1,0:T(8,128)} fusion(bf16[4,1024,2048]{2,1,0:T(8,128)(2,1)} %get-tuple-element.58, bf16[4,1024,128]{2,1,0:T(8,128)(2,1)S(1)} %bitcast.35), kind=kOutput, calls=%fused_computation.9 | convolution fusion | flops 2147483648 | bytes 18874368 | tf_op jit(solution)/shard_map/kbc,kbd->cd/dot_general | solution.py:33
  243.5 50.6 %all-reduce.8.cloned.1.call-done = f32[2048,128]{1,0:T(8,128)} async-done(((f32[2048,128]{1,0:T(8,128)}), f32[2048,128]{1,0:T(8,128)}) %all-reduce.8.cloned.1.call-update) | async-done | bytes 1048592 | tf_op jit(solution)/shard_map/psum | solution.py:57
  294.0 9.8 %convolution_bitcast_fusion = f32[4096,128]{0,1:T(8,128)} fusion(bf16[2048,4096]{1,0:T(8,128)(2,1)} %param.10, f32[2048,128]{1,0:T(8,128)} %all-reduce.8.cloned.1.call-done), kind=kOutput, calls=%fused_computation.8 | convolution fusion | flops 2148007936 | bytes 19922944 | tf_op jit(solution)/shard_map/dot_general | solution.py:61
  304.8 39.4 %reduce-scatter.2.cloned.1.call-done = f32[512,128]{0,1:T(8,128)} async-done(((f32[4096,128]{0,1:T(8,128)}), f32[512,128]{0,1:T(8,128)}) %reduce-scatter.2.cloned.1.call-update) | async-done | bytes 262160 | tf_op jit(solution)/shard_map/reduce_scatter | solution.py:60
  344.2 1.6 multiply_reduce_fusion.2
  346.0 39.6 %all-reduce = (f32[]{:T(128)}, f32[]{:T(128)}) all-reduce(f32[]{:T(128)} %multiply_reduce_fusion.3, f32[]{:T(128)} %multiply_reduce_fusion.2), channel_id=1, replica_groups=mesh['rows'=4,'cent'=8] {'rows','cent'}, use_global_device_ids=true, to_apply=%region_1.2 | all-reduce | flops 2 | bytes 16 | tf_op jit(solution)/shard_map/psum | solution.py:69
  386.9 1.6 multiply_reduce_fusion.1
  388.6 41.3 %psum.55 = f32[]{:T(128)} all-reduce(f32[]{:T(128)} %get-tuple-element.74), channel_id=1, replica_groups=mesh['rows'=4,'cent'=8] {'rows','cent'}, use_global_device_ids=true, to_apply=%region_14.15 | all-reduce | flops 1 | bytes 8 | tf_op jit(solution)/shard_map/psum | solution.py:75
  432.1 0.8 copy.17
  (29 shorter events, 5.3 us)
Async XLA Ops:
  8.0 64.9 %all-reduce.6.cloned.1.call-start = ((), (), s32[]{:S(2)}) async-start(), calls=%async_computation.1 | async-start | bytes 2097152 | tf_op jit(solution)/shard_map/psum | solution.py:43
  18.1 101.4 %all-gather.2.cloned.1.call-start = ((), (), s32[]{:S(2)}) async-start(), calls=%async_computation.2 | async-start | bytes 1179648 | tf_op jit(solution)/shard_map/all_gather | solution.py:48
  19.8 274.2 %all-reduce.8.cloned.1.call-start = ((), (), s32[]{:S(2)}) async-start(), calls=%async_computation.3 | async-start | bytes 2097152 | tf_op jit(solution)/shard_map/psum | solution.py:57
  243.4 60.5 %copy-start = (f32[512,128]{1,0:T(8,128)S(1)}, f32[512,128]{1,0:T(8,128)}, u32[]{:S(2)}) copy-start(f32[512,128]{1,0:T(8,128)} %param.13) | copy-start | bytes 786436
  243.4 60.7 %copy-start.1 = (f32[512,128]{1,0:T(8,128)S(1)}, f32[512,128]{1,0:T(8,128)}, u32[]{:S(2)}) copy-start(f32[512,128]{1,0:T(8,128)} %param.12) | copy-start | bytes 786436
  243.4 102.5 %copy-start.2 = (f32[512,128]{1,0:T(8,128)S(1)}, f32[512,128]{1,0:T(8,128)}, u32[]{:S(2)}) copy-start(f32[512,128]{1,0:T(8,128)} %param.11) | copy-start | bytes 786436
  243.4 100.8 %reduce-scatter.2.cloned.1.call-start = ((), (), s32[]{:S(2)}) async-start(), calls=%async_computation.4 | async-start | bytes 2359296 | tf_op jit(solution)/shard_map/reduce_scatter | solution.py:60
Sparse Core Ops, SparseCore 0:
  18.2 54.6 all-reduce.5
  243.5 50.4 all-reduce.7
Sparse Core Ops, SparseCore 1:
  21.1 25.9 all-gather.1
  304.0 40.2 reduce-scatter.1
where the time goes:
time: 442 us; the launch traced here: 441 us
  blocking collectives  179 us (40%)
  waiting for transfers between devices  143 us (32%)
  matrix products  79.7 us (18%)
  between operations  18.3 us (4%)
  other arithmetic  10.7 us (2%)
  local copies, waits for them, and re-layouts  10.2 us (2%)
    psum x1, blocking collectives, line_sum(): return lax.psum(part, 'cent').astype(jnp.bfloat16)  56.6 us
    psum x1, waiting for transfers between devices, on_device(): centres = lax.psum(picked, 'rows')  53 us
    psum x1, waiting for transfers between devices, on_device(): grad = lax.psum(grad_part, 'rows')  50.6 us
    dot_general x4, matrix products, kernel_tile(): jnp.dot(block_rows, centres.T, precision=lax.Precision.HIGHEST, preferred...  44.2 us
    psum x1, blocking collectives, on_device(): coef_field = lax.psum(partial_field, 'rows').astype(jnp.bfloat16)  41.5 us
    psum x1, blocking collectives, on_device(): lax.psum(jnp.sum(residual_next * residual_next), ('rows', 'cent'))  41.3 us
    psum x1, blocking collectives, on_device(): lax.psum((jnp.sum(residual * residual), jnp.sum(direction * image)), ('ro...  39.6 us
    reduce_scatter x1, waiting for transfers between devices, on_device(): lax.psum_scatter(lax.dot_general(columns, grad_low, (((0,), (0,)), ((), (...  39.4 us
  transfers between devices with their start and end apart: 4, of which 3 were waited for; matrix products, arithmetic and copies ran while one was open for 11% of the time, Pallas kernels for 0%

commit v1 on v0

--- a/solution.py
+++ b/solution.py
@@ -67,7 +67,7 @@
     )
     image = image + ridge_weight * direction
     norm_old, curvature = lax.psum(
-        (jnp.sum(residual * residual), jnp.sum(direction * image)), ("rows", "cent")
+        lax.psum((jnp.sum(residual * residual), jnp.sum(direction * image)), "cent"), "rows"
     )
     step_size = norm_old / curvature
     coef_next = coefficients + step_size * direction

time: 442 us -> 424 us (0.959)
  blocking collectives: 179 us -> 161 us
    psum x1 -> x2, blocking collectives: 39.6 us -> 25.4 us  [the longest x1 13.1 us: on_device(): lax.psum((jnp.sum(residual * residual), jnp.sum(direction * image)), 'cent')]
  transfers between devices with their start and end apart: 4 -> 4, of which waited for: 3 -> 3; matrix products, arithmetic and copies ran while one was open for 11% -> 12% of each run, Pallas kernels for 0% -> 0%
where the time goes in v1:
time: 424 us; the launch traced here: 423 us
  blocking collectives  161 us (38%)
  waiting for transfers between devices  143 us (34%)
  matrix products  79.7 us (19%)
  between operations  18.3 us (4%)
  other arithmetic  10.7 us (3%)
  local copies, waits for them, and re-layouts  10.2 us (2%)
    psum x1, blocking collectives, line_sum(): return lax.psum(part, 'cent').astype(jnp.bfloat16)  56.6 us
    psum x1, waiting for transfers between devices, on_device(): centres = lax.psum(picked, 'rows')  53 us
    psum x1, waiting for transfers between devices, on_device(): grad = lax.psum(grad_part, 'rows')  50.6 us
    dot_general x4, matrix products, kernel_tile(): jnp.dot(block_rows, centres.T, precision=lax.Precision.HIGHEST, preferred...  44.2 us
    psum x1, blocking collectives, on_device(): coef_field = lax.psum(partial_field, 'rows').astype(jnp.bfloat16)  41.5 us
    reduce_scatter x1, waiting for transfers between devices, on_device(): lax.psum_scatter(lax.dot_general(columns, grad_low, (((0,), (0,)), ((), (...  39.4 us
    psum x1, blocking collectives, on_device(): lax.psum(jnp.sum(residual_next * residual_next), ('rows', 'cent'))  37 us
    psum x1, blocking collectives, on_device(): lax.psum((jnp.sum(residual * residual), jnp.sum(direction * image)), 'cent')  13.1 us
  transfers between devices with their start and end apart: 4, of which 3 were waited for; matrix products, arithmetic and copies ran while one was open for 12% of the time, Pallas kernels for 0%

profile of v1, /device:TPU:0, one launch (start us, length us, event | category | flops | bytes accessed | tf_op | source)
XLA Modules:
  0.0 422.7 jit_solution(13444943774348991936)
XLA Ops:
  9.5 1.8 copy.9
  11.3 5.5 %gather_fusion = f32[2048,64]{1,0:T(8,128)S(1)} fusion(f32[4096,64]{1,0:T(8,128)S(1)} %copy.9, s32[2048]{0:T(1024)S(1)} %fusion.8), kind=kCustom, calls=%fused_computation | custom fusion | bytes 1056768 | tf_op jit(solution)/shard_map/gather | solution.py:42
  16.8 1.3 broadcast_multiply_fusion
  18.2 1.6 convert_element_type.21
  19.9 53.0 %all-reduce.7.cloned.1.call-done = f32[2048,64]{1,0:T(8,128)} async-done(((f32[2048,64]{1,0:T(8,128)}), f32[2048,64]{1,0:T(8,128)}) %all-reduce.7.cloned.1.call-update) | async-done | bytes 524304 | tf_op jit(solution)/shard_map/psum | solution.py:43
  72.9 1.6 multiply_reduce_fusion
  74.5 45.0 %while.12 = (s32[]{:T(128)}, bf16[4,1024,2048]{2,1,0:T(8,128)(2,1)}, f32[4,1024,64]{2,1,0:T(8,128)S(1)}, f32[2048]{0:T(1024)S(1)}, f32[2048,64]{1,0:T(8,128)}, /*index=5*/s32[]{:T(128)}) while((s32[]{:T(128)}, bf16[4,1024,2048]{2,1,0:T(8,128)(2,1)}, f32[4,1024,64]{2,1,0:T(8,128)S(1)}, f32[2048]{0:T(1024)S(1)}, f32[2048,64]{1,0:T(8,128)}, ...), condition=%wide.region_7.8_spmd, body=%wide.region_5.7_spmd.sunk | while | flops 1621228544 | bytes 6046793 | solution.py:27
  74.7 11.0 %bitcast_dynamic-update-slice_fusion.2 = bf16[4,1024,2048]{2,1,0:T(8,128)(2,1)} fusion(bf16[4,1024,2048]{2,1,0:T(8,128)(2,1)} %get-tuple-element.118, s32[]{:T(128)} %get-tuple-element.117, f32[2048,64]{1,0:T(8,128)} %get-tuple-element.127, f32[2048]{0:T(1024)S(1)} %get-tuple-element.126, f32[1024]{0:T(1024)S(1)} %fusion.23, ...), kind=kOutput, calls=%fused_computation.2.clone.1 | convolution fusion | flops 1621098496 | bytes 5780480 | tf_op jit(solution)/shard_map/while/body/eval_jaxpr/dot_general | solution.py:15
  85.9 11.1 %bitcast_dynamic-update-slice_fusion.2 = bf16[4,1024,2048]{2,1,0:T(8,128)(2,1)} fusion(bf16[4,1024,2048]{2,1,0:T(8,128)(2,1)} %get-tuple-element.118, s32[]{:T(128)} %get-tuple-element.117, f32[2048,64]{1,0:T(8,128)} %get-tuple-element.127, f32[2048]{0:T(1024)S(1)} %get-tuple-element.126, f32[1024]{0:T(1024)S(1)} %fusion.23, ...), kind=kOutput, calls=%fused_computation.2.clone.1 | convolution fusion | flops 1621098496 | bytes 5780480 | tf_op jit(solution)/shard_map/while/body/eval_jaxpr/dot_general | solution.py:15
  97.2 11.0 %bitcast_dynamic-update-slice_fusion.2 = bf16[4,1024,2048]{2,1,0:T(8,128)(2,1)} fusion(bf16[4,1024,2048]{2,1,0:T(8,128)(2,1)} %get-tuple-element.118, s32[]{:T(128)} %get-tuple-element.117, f32[2048,64]{1,0:T(8,128)} %get-tuple-element.127, f32[2048]{0:T(1024)S(1)} %get-tuple-element.126, f32[1024]{0:T(1024)S(1)} %fusion.23, ...), kind=kOutput, calls=%fused_computation.2.clone.1 | convolution fusion | flops 1621098496 | bytes 5780480 | tf_op jit(solution)/shard_map/while/body/eval_jaxpr/dot_general | solution.py:15
  108.4 11.1 %bitcast_dynamic-update-slice_fusion.2 = bf16[4,1024,2048]{2,1,0:T(8,128)(2,1)} fusion(bf16[4,1024,2048]{2,1,0:T(8,128)(2,1)} %get-tuple-element.118, s32[]{:T(128)} %get-tuple-element.117, f32[2048,64]{1,0:T(8,128)} %get-tuple-element.127, f32[2048]{0:T(1024)S(1)} %get-tuple-element.126, f32[1024]{0:T(1024)S(1)} %fusion.23, ...), kind=kOutput, calls=%fused_computation.2.clone.1 | convolution fusion | flops 1621098496 | bytes 5780480 | tf_op jit(solution)/shard_map/while/body/eval_jaxpr/dot_general | solution.py:15
  119.5 8.4 %fusion.10 = f32[2048,128]{1,0:T(8,128)S(1)} fusion(bf16[2048,4096]{1,0:T(8,128)(2,1)} %param.10, bf16[4096,128]{1,0:T(8,128)(2,1)} %all-gather.2.cloned.1.call-done), kind=kOutput, calls=%fused_computation.28 | convolution fusion | flops 2147483648 | bytes 18874368 | tf_op jit(solution)/shard_map/dot_general | solution.py:46
  127.9 41.5 %all-reduce.10 = bf16[2048,128]{1,0:T(8,128)(2,1)S(1)} all-reduce(f32[2048,128]{1,0:T(8,128)S(1)} %fusion.10), channel_id=1, replica_groups=mesh['rows'=4,'cent'=8] {'rows'}, use_global_device_ids=true, to_apply=%region_8.9 | all-reduce | flops 262144 | bytes 1572864 | tf_op jit(solution)/shard_map/psum | solution.py:51
  169.5 8.2 %fusion.4 = f32[4,1024,128]{2,1,0:T(8,128)S(1)} fusion(bf16[4,1024,2048]{2,1,0:T(8,128)(2,1)} %get-tuple-element.58, bf16[2048,128]{1,0:T(8,128)(2,1)S(1)} %all-reduce.10), kind=kOutput, calls=%fused_computation.12 | convolution fusion | flops 2147483648 | bytes 19398656 | tf_op jit(solution)/shard_map/kbc,cd->kbd/dot_general | solution.py:28
  177.6 56.6 %all-reduce.11 = bf16[4096,128]{1,0:T(8,128)(2,1)S(1)} all-reduce(f32[4096,128]{1,0:T(8,128)S(1)} %bitcast.34), channel_id=1, replica_groups=mesh['rows'=4,'cent'=8] {'cent'}, use_global_device_ids=true, to_apply=%region_9.10 | all-reduce | flops 524288 | bytes 3145728 | tf_op jit(solution)/shard_map/psum | solution.py:54
  234.2 9.2 %convolution_bitcast_fusion.1 = f32[2048,128]{1,0:T(8,128)} fusion(bf16[4,1024,2048]{2,1,0:T(8,128)(2,1)} %get-tuple-element.58, bf16[4,1024,128]{2,1,0:T(8,128)(2,1)S(1)} %bitcast.35), kind=kOutput, calls=%fused_computation.9 | convolution fusion | flops 2147483648 | bytes 18874368 | tf_op jit(solution)/shard_map/kbc,kbd->cd/dot_general | solution.py:33
  243.5 50.6 %all-reduce.9.cloned.1.call-done = f32[2048,128]{1,0:T(8,128)} async-done(((f32[2048,128]{1,0:T(8,128)}), f32[2048,128]{1,0:T(8,128)}) %all-reduce.9.cloned.1.call-update) | async-done | bytes 1048592 | tf_op jit(solution)/shard_map/psum | solution.py:57
  294.0 9.8 %convolution_bitcast_fusion = f32[4096,128]{0,1:T(8,128)} fusion(bf16[2048,4096]{1,0:T(8,128)(2,1)} %param.10, f32[2048,128]{1,0:T(8,128)} %all-reduce.9.cloned.1.call-done), kind=kOutput, calls=%fused_computation.8 | convolution fusion | flops 2148007936 | bytes 19922944 | tf_op jit(solution)/shard_map/dot_general | solution.py:61
  304.8 39.4 %reduce-scatter.2.cloned.1.call-done = f32[512,128]{0,1:T(8,128)} async-done(((f32[4096,128]{0,1:T(8,128)}), f32[512,128]{0,1:T(8,128)}) %reduce-scatter.2.cloned.1.call-update) | async-done | bytes 262160 | tf_op jit(solution)/shard_map/reduce_scatter | solution.py:60
  344.2 1.6 multiply_reduce_fusion.2
  346.0 13.1 %all-reduce = (f32[]{:T(128)}, f32[]{:T(128)}) all-reduce(f32[]{:T(128)} %multiply_reduce_fusion.3, f32[]{:T(128)} %multiply_reduce_fusion.2), channel_id=1, replica_groups=mesh['rows'=4,'cent'=8] {'cent'}, use_global_device_ids=true, to_apply=%region_1.2 | all-reduce | flops 2 | bytes 16 | tf_op jit(solution)/shard_map/psum | solution.py:70
  359.1 12.3 %all-reduce.1 = (f32[]{:T(128)}, f32[]{:T(128)}) all-reduce(f32[]{:T(128)} %get-tuple-element.72, f32[]{:T(128)} %get-tuple-element.73), channel_id=1, replica_groups=mesh['rows'=4,'cent'=8] {'rows'}, use_global_device_ids=true, to_apply=%region_2.3 | all-reduce | flops 2 | bytes 16 | tf_op jit(solution)/shard_map/psum | solution.py:69
  372.7 1.6 multiply_reduce_fusion.1
  374.4 37.0 %psum.71 = f32[]{:T(128)} all-reduce(f32[]{:T(128)} %get-tuple-element.76), channel_id=1, replica_groups=mesh['rows'=4,'cent'=8] {'rows','cent'}, use_global_device_ids=true, to_apply=%region_16.17 | all-reduce | flops 1 | bytes 8 | tf_op jit(solution)/shard_map/psum | solution.py:75
  (30 shorter events, 6.1 us)
Async XLA Ops:
  8.0 64.9 %all-reduce.7.cloned.1.call-start = ((), (), s32[]{:S(2)}) async-start(), calls=%async_computation.1 | async-start | bytes 2097152 | tf_op jit(solution)/shard_map/psum | solution.py:43
  18.1 101.4 %all-gather.2.cloned.1.call-start = ((), (), s32[]{:S(2)}) async-start(), calls=%async_computation.2 | async-start | bytes 1179648 | tf_op jit(solution)/shard_map/all_gather | solution.py:48
  19.8 274.2 %all-reduce.9.cloned.1.call-start = ((), (), s32[]{:S(2)}) async-start(), calls=%async_computation.3 | async-start | bytes 2097152 | tf_op jit(solution)/shard_map/psum | solution.py:57
  243.4 60.5 %copy-start = (f32[512,128]{1,0:T(8,128)S(1)}, f32[512,128]{1,0:T(8,128)}, u32[]{:S(2)}) copy-start(f32[512,128]{1,0:T(8,128)} %param.13) | copy-start | bytes 786436
  243.4 60.7 %copy-start.1 = (f32[512,128]{1,0:T(8,128)S(1)}, f32[512,128]{1,0:T(8,128)}, u32[]{:S(2)}) copy-start(f32[512,128]{1,0:T(8,128)} %param.12) | copy-start | bytes 786436
  243.4 102.5 %copy-start.2 = (f32[512,128]{1,0:T(8,128)S(1)}, f32[512,128]{1,0:T(8,128)}, u32[]{:S(2)}) copy-start(f32[512,128]{1,0:T(8,128)} %param.11) | copy-start | bytes 786436
  243.4 100.8 %reduce-scatter.2.cloned.1.call-start = ((), (), s32[]{:S(2)}) async-start(), calls=%async_computation.4 | async-start | bytes 2359296 | tf_op jit(solution)/shard_map/reduce_scatter | solution.py:60
Sparse Core Ops, SparseCore 0:
  18.2 54.6 all-reduce.6
  243.5 50.4 all-reduce.8
Sparse Core Ops, SparseCore 1:
  21.1 25.9 all-gather.1
  304.0 40.2 reduce-scatter.1
